TPU v7x, 32 devices: a whole 2x2x4 slice. The times are simulated.
32 devices in a mesh: expert: 16 (over z, y, x), tok: 2 (over core).
Axes of the slice: x: 2, y: 2, z: 4, core: 2. Of those that a mesh axis runs over, the one named last changes fastest.
Arguments:
- tokens: bfloat16 [2048, 3584], P(('expert', 'tok')), may hold values from -6 to 6
- routes: int32 [2048, 8], P(('expert', 'tok')), may hold values from 0 to 15, all different within a row; in each aligned block of 64 rows (0 to 63, 64 to 127, ...) at most 36 rows name the same one
- gates: float32 [2048, 8], P(('expert', 'tok')), may hold values from 0.05 to 1
- upstream: bfloat16 [2048, 3584], P(('expert', 'tok')), may hold values from -6 to 6
- w_up: bfloat16 [16, 3584, 1024], P('expert', None, 'tok'), may hold values from -0.09375 to 0.09375
- w_down: bfloat16 [16, 1024, 3584], P('expert', 'tok'), may hold values from -0.1875 to 0.1875
Outputs:
- mixed: bfloat16 [2048, 3584], P(('expert', 'tok'))
- d_tokens: bfloat16 [2048, 3584], P(('expert', 'tok'))
- d_gates: float32 [2048, 8], P(('expert', 'tok'))
- grad_up: bfloat16 [16, 3584, 1024], P('expert', None, 'tok')
- grad_down: bfloat16 [16, 1024, 3584], P('expert', 'tok')
Inputs may be any that keep to these rules, and one draw needn't show every extreme that they name: `routes`: each token names 8 different experts. At most 36 of the 64 tokens of one device name the same expert, and in every draw the tokens of some device name some expert exactly 36 times.
All inputs are finite; a program needn't handle non-finite values.
Results may differ from a plain program's by a relative error of at most 0.0065.
Values may be sent and summed in bfloat16 or wider, within the bound.
A program may use at most 192 MiB of HBM per device.

v0:
```python
import jax
import jax.numpy as jnp
from jax import lax
from jax.sharding import PartitionSpec as P

GELU_C = 0.7978845608028654
GELU_A = 0.044715


def gelu_value(hidden):
    inner_arg = GELU_C * (hidden + GELU_A * hidden * hidden * hidden)
    return 0.5 * hidden * (1.0 + jnp.tanh(inner_arg))


def gelu_slope(hidden):
    tangent = jnp.tanh(GELU_C * (hidden + GELU_A * hidden * hidden * hidden))
    return 0.5 * (1.0 + tangent) + 0.5 * hidden * (1.0 - tangent * tangent) * GELU_C * (
        1.0 + 3.0 * GELU_A * hidden * hidden
    )


def expert_rows(rows_x, rows_grad, up_local, down_local):
    hidden = jnp.dot(rows_x, up_local, preferred_element_type=jnp.float32)
    active = gelu_value(hidden).astype(jnp.bfloat16)
    out_part = jnp.dot(active, down_local, preferred_element_type=jnp.float32)
    d_active = lax.dot_general(
        rows_grad, down_local, (((1,), (1,)), ((), ())), preferred_element_type=jnp.float32
    )
    d_hidden = (d_active * gelu_slope(hidden)).astype(jnp.bfloat16)
    dx_part = lax.dot_general(
        d_hidden, up_local, (((1,), (1,)), ((), ())), preferred_element_type=jnp.float32
    )
    grad_down = lax.dot_general(
        active, rows_grad, (((0,), (0,)), ((), ())), preferred_element_type=jnp.float32
    )
    grad_up = lax.dot_general(
        rows_x, d_hidden, (((0,), (0,)), ((), ())), preferred_element_type=jnp.float32
    )
    return (out_part, dx_part, grad_up, grad_down)


def routed_shards(tokens, routes, gates, upstream, w_up, w_down):
    tok_rows, feature_width = tokens.shape
    top_count = routes.shape[1]
    owners = lax.axis_size("expert")
    pair_count = lax.axis_size("tok")
    capacity = tok_rows * top_count // owners + max(1, tok_rows * top_count // (8 * owners))
    assigned = routes.reshape(-1)
    labels = jnp.arange(owners, dtype=jnp.int32)
    onehot = (assigned[:, None] == labels[None, :]).astype(jnp.int32)
    earlier = jnp.cumsum(onehot, axis=0) - onehot
    slot_rank = jnp.sum(earlier * onehot, axis=1)
    slot_of = assigned * capacity + slot_rank
    slot_ids = jnp.arange(owners * capacity, dtype=jnp.int32)
    matches = (slot_of[None, :] == slot_ids[:, None]).astype(jnp.int32)
    filled = jnp.sum(matches, axis=1) > 0
    source = jnp.sum(matches * jnp.arange(assigned.shape[0], dtype=jnp.int32)[None, :], axis=1)
    token_ids = source // top_count
    send_x = jnp.where(filled[:, None], tokens[token_ids], jnp.zeros((), jnp.bfloat16))
    gate_rows = jnp.where(filled, gates.reshape(-1)[source], jnp.zeros((), jnp.float32))
    send_grad = (gate_rows[:, None] * upstream[token_ids].astype(jnp.float32)).astype(jnp.bfloat16)
    send_x = send_x.reshape(owners, capacity, feature_width)
    send_grad = send_grad.reshape(owners, capacity, feature_width)
    recv_x, recv_grad = (
        lax.all_to_all(send_x, "expert", split_axis=0, concat_axis=0, tiled=True),
        lax.all_to_all(send_grad, "expert", split_axis=0, concat_axis=0, tiled=True),
    )
    both_x, both_grad = (
        lax.all_gather(recv_x[None], "tok", axis=0, tiled=True),
        lax.all_gather(recv_grad[None], "tok", axis=0, tiled=True),
    )
    rows_x = both_x.reshape(-1, feature_width)
    rows_grad = both_grad.reshape(-1, feature_width)
    out_part, dx_part, grad_up, grad_down = expert_rows(rows_x, rows_grad, w_up[0], w_down[0])
    shaped_out = out_part.reshape(pair_count, owners, capacity, feature_width)
    shaped_dx = dx_part.reshape(pair_count, owners, capacity, feature_width)
    summed_out, summed_dx = (
        lax.psum_scatter(shaped_out, "tok", scatter_dimension=0, tiled=True),
        lax.psum_scatter(shaped_dx, "tok", scatter_dimension=0, tiled=True),
    )
    home_out, home_dx = (
        lax.all_to_all(
            summed_out[0].astype(jnp.bfloat16), "expert", split_axis=0, concat_axis=0, tiled=True
        ),
        lax.all_to_all(
            summed_dx[0].astype(jnp.bfloat16), "expert", split_axis=0, concat_axis=0, tiled=True
        ),
    )
    out_pairs = (
        home_out.reshape(owners * capacity, feature_width)[slot_of]
        .reshape(tok_rows, top_count, feature_width)
        .astype(jnp.float32)
    )
    dx_pairs = (
        home_dx.reshape(owners * capacity, feature_width)[slot_of]
        .reshape(tok_rows, top_count, feature_width)
        .astype(jnp.float32)
    )
    mixed_out = jnp.sum(gates[:, :, None] * out_pairs, axis=1).astype(jnp.bfloat16)
    d_gates = jnp.sum(upstream.astype(jnp.float32)[:, None, :] * out_pairs, axis=2)
    d_tokens = jnp.sum(dx_pairs, axis=1).astype(jnp.bfloat16)
    return (
        mixed_out,
        d_tokens,
        d_gates,
        grad_up.astype(jnp.bfloat16)[None],
        grad_down.astype(jnp.bfloat16)[None],
    )


def dense_shards(tokens, routes, gates, upstream, w_up, w_down):
    tok_rows, width = tokens.shape
    owners = lax.axis_size("expert")
    half = w_up.shape[2]
    swap = ((0, 1), (1, 0))
    up_local, down_local = (w_up[0], w_down[0])
    up_full = jnp.concatenate([up_local, lax.ppermute(up_local, "tok", swap)], axis=1)
    down_full = jnp.concatenate([down_local, lax.ppermute(down_local, "tok", swap)], axis=0)
    named = routes[:, :, None] == jnp.arange(owners, dtype=jnp.int32)
    gate_of = jnp.sum(jnp.where(named, gates[:, :, None], 0.0), axis=1)
    gate = lax.all_to_all(gate_of.T, "expert", split_axis=0, concat_axis=0, tiled=True)
    gate = gate.reshape(-1)[:, None]
    all_x = lax.all_gather(tokens, "expert", axis=0, tiled=True)
    all_u = lax.all_gather(upstream, "expert", axis=0, tiled=True)
    hidden = jnp.dot(all_x, up_full, preferred_element_type=jnp.float32)
    gated = (gate * gelu_value(hidden)).astype(jnp.bfloat16)
    mixed_part = jnp.dot(gated, down_full, preferred_element_type=jnp.float32)
    mixed = lax.psum_scatter(
        mixed_part.astype(jnp.bfloat16), "expert", scatter_dimension=0, tiled=True
    )
    back = lax.dot_general(
        all_u, down_full, (((1,), (1,)), ((), ())), preferred_element_type=jnp.float32
    )
    inner = jnp.sum(gelu_value(hidden) * back, axis=1)
    d_hidden = (gate * back * gelu_slope(hidden)).astype(jnp.bfloat16)
    dx_part = lax.dot_general(
        d_hidden, up_full, (((1,), (1,)), ((), ())), preferred_element_type=jnp.float32
    )
    d_tokens = lax.psum_scatter(
        dx_part.astype(jnp.bfloat16), "expert", scatter_dimension=0, tiled=True
    )
    home = lax.all_to_all(
        inner.reshape(owners, tok_rows), "expert", split_axis=0, concat_axis=0, tiled=True
    )
    d_gates = jnp.sum(jnp.where(named, home.T[:, None, :], 0.0), axis=2)

    def outer(rows, columns):
        return lax.dot_general(
            rows, columns, (((0,), (0,)), ((), ())), preferred_element_type=jnp.float32
        )

    down_far = outer(gated[:, half:], all_u).astype(jnp.bfloat16)
    up_far = outer(all_x, d_hidden[:, half:]).astype(jnp.bfloat16)
    down_near = outer(gated[:, :half], all_u)
    up_near = outer(all_x, d_hidden[:, :half])
    grad_down = down_near + lax.ppermute(down_far, "tok", swap).astype(jnp.float32)
    grad_up = up_near + lax.ppermute(up_far, "tok", swap).astype(jnp.float32)
    return (
        mixed,
        d_tokens,
        d_gates,
        grad_up.astype(jnp.bfloat16)[None],
        grad_down.astype(jnp.bfloat16)[None],
    )


def shards(tokens, routes, gates, upstream, w_up, w_down):
    dense = 2 * routes.shape[1] >= lax.axis_size("expert") and lax.axis_size("tok") == 2
    body = dense_shards if dense else routed_shards
    return body(tokens, routes, gates, upstream, w_up, w_down)


def solution(mesh):
    return jax.shard_map(
        shards,
        mesh=mesh,
        in_specs=(
            P(("expert", "tok"), None),
            P(("expert", "tok"), None),
            P(("expert", "tok"), None),
            P(("expert", "tok"), None),
            P("expert", None, "tok"),
            P("expert", "tok", None),
        ),
        out_specs=(
            P(("expert", "tok"), None),
            P(("expert", "tok"), None),
            P(("expert", "tok"), None),
            P("expert", None, "tok"),
            P("expert", "tok", None),
        ),
        check_vma=False,
    )
```

profile of v0, /device:TPU:10, one launch (start us, length us, event | category | flops | bytes accessed | tf_op | source)
XLA Modules:
  0.0 600.3 jit_solution(6524580034297987019)
XLA Ops:
  7.2 0.7 all-gather.3.cloned.1.call-update
  7.9 0.7 all-gather.5.cloned.1.call-update
  8.8 0.5 collective-permute-start.1
  9.3 6.2 %collective-permute-done = bf16[3584,512]{1,0:T(8,128)(2,1)} collective-permute-done((bf16[3584,512]{1,0:T(8,128)(2,1)}, bf16[3584,512]{1,0:T(8,128)(2,1)}, u32[]{:S(2)}, u32[]{:S(2)}) %collective-permute-start) | collective-permute-done | bytes 3670048 | tf_op jit(solution)/shard_map/ppermute | solution.py:117
  15.5 98.8 %all-gather.3.cloned.1.call-done = bf16[1024,3584]{1,0:T(8,128)(2,1)} async-done(((bf16[64,3584]{1,0:T(8,128)(2,1)}), bf16[1024,3584]{1,0:T(8,128)(2,1)}) %all-gather.3.cloned.1.call-update) | async-done | bytes 7340048 | tf_op jit(solution)/shard_map/all_gather | solution.py:123
  114.3 13.6 %fusion.4 = f32[1024,1024]{1,0:T(8,128)} fusion(bf16[1024,3584]{1,0:T(8,128)(2,1)} %all-gather.3.cloned.1.call-done, bf16[3584,512]{1,0:T(8,128)(2,1)} %collective-permute-done, bf16[3584,512]{1,0:T(8,128)(2,1)} %bitcast.60), kind=kOutput, calls=%fused_computation.14 | convolution fusion | flops 7530872832 | bytes 18874368 | tf_op jit(solution)/shard_map/dot_general | solution.py:125
  127.9 90.8 %all-gather.5.cloned.1.call-done = bf16[1024,3584]{1,0:T(8,128)(2,1)} async-done(((bf16[64,3584]{1,0:T(8,128)(2,1)}), bf16[1024,3584]{1,0:T(8,128)(2,1)}) %all-gather.5.cloned.1.call-update) | async-done | bytes 7340048 | tf_op jit(solution)/shard_map/all_gather | solution.py:124
  218.7 15.0 %fusion.12 = (f32[1024]{0:T(1024)S(1)}, f32[1024,1024]{1,0:T(8,128)}) fusion(f32[1024,1024]{1,0:T(8,128)} %fusion.4, bf16[1024,3584]{1,0:T(8,128)(2,1)} %all-gather.5.cloned.1.call-done, bf16[512,3584]{1,0:T(8,128)(2,1)} %collective-permute-done.1, bf16[512,3584]{1,0:T(8,128)(2,1)} %bitcast.63), kind=kOutput, calls=%fused_computation.24 | convolution fusion | flops 7541357568 | bytes 23072768 | tf_op jit(solution)/shard_map/dot_general | solution.py:131
  233.7 10.0 %all_to_all.21 = f32[16,1,64]{2,1,0:T(1,128)S(1)} all-to-all(f32[16,1,64]{2,1,0:T(1,128)S(1)} %bitcast.56), channel_id=1, replica_groups=mesh['expert'=16,'tok'=2] {'expert'}, dimensions={0} | all-to-all | bytes 8192 | tf_op jit(solution)/shard_map/all_to_all | solution.py:142
  243.8 0.6 select_reduce_fusion
  244.4 9.8 %all_to_all.22 = f32[16,1,64]{2,1,0:T(1,128)S(1)} all-to-all(f32[16,1,64]{2,1,0:T(1,128)S(1)} %bitcast.55), channel_id=1, replica_groups=mesh['expert'=16,'tok'=2] {'expert'}, dimensions={0} | all-to-all | bytes 8192 | tf_op jit(solution)/shard_map/all_to_all | solution.py:121
  254.2 0.5 broadcast.46
  254.7 0.7 reduce.3
  255.5 5.6 fusion.11
  261.1 1.3 copy-done
  262.4 12.0 %convolution_convert_fusion = bf16[1024,3584]{1,0:T(8,128)(2,1)} fusion(bf16[1024,1024]{0,1:T(8,128)(2,1)S(1)} %get-tuple-element.27, bf16[3584,512]{1,0:T(8,128)(2,1)} %collective-permute-done, bf16[3584,512]{1,0:T(8,128)(2,1)S(1)} %bitcast.61), kind=kOutput, calls=%fused_computation | convolution fusion | flops 7534542848 | bytes 16777216 | tf_op jit(solution)/shard_map/dot_general | solution.py:136
  274.6 13.0 %convolution_convert_fusion.1 = bf16[1024,3584]{1,0:T(8,128)(2,1)} fusion(bf16[1024,1024]{0,1:T(8,128)(2,1)S(1)} %get-tuple-element.28, bf16[512,3584]{1,0:T(8,128)(2,1)} %collective-permute-done.1, bf16[512,3584]{1,0:T(8,128)(2,1)} %bitcast.64), kind=kOutput, calls=%fused_computation.1 | convolution fusion | flops 7534542848 | bytes 16777216 | tf_op jit(solution)/shard_map/dot_general | solution.py:127
  287.7 7.5 %fusion.1 = bf16[3584,512]{0,1:T(8,128)(2,1)S(1)} fusion(bf16[1024,3584]{1,0:T(8,128)(2,1)} %all-gather.3.cloned.1.call-done, bf16[1024,1024]{0,1:T(8,128)(2,1)} %copy-done), kind=kOutput, calls=%fused_computation.11 | convolution fusion | flops 3759931392 | bytes 12058624 | tf_op jit(solution)/shard_map/dot_general | solution.py:148
  295.4 8.7 %convolution_convert_fusion.2 = bf16[512,3584]{1,0:T(8,128)(2,1)} fusion(bf16[1024,3584]{1,0:T(8,128)(2,1)} %all-gather.5.cloned.1.call-done, bf16[1024,1024]{0,1:T(8,128)(2,1)S(1)} %get-tuple-element.28), kind=kOutput, calls=%fused_computation.9 | convolution fusion | flops 3759931392 | bytes 12058624 | tf_op jit(solution)/shard_map/dot_general | solution.py:148
  304.4 5.4 fusion.2
  309.8 5.9 copy.25
  315.7 9.1 %fusion.14 = bf16[1,512,3584]{2,1,0:T(8,128)(2,1)} fusion(bf16[512,3584]{1,0:T(8,128)(2,1)} %collective-permute-done.3, bf16[1024,3584]{1,0:T(8,128)(2,1)} %all-gather.5.cloned.1.call-done, bf16[1024,1024]{0,1:T(8,128)(2,1)S(1)} %get-tuple-element.28), kind=kOutput, calls=%fused_computation.28 | convolution fusion | flops 3763601408 | bytes 15728640 | tf_op jit(solution)/shard_map/dot_general | solution.py:148
  324.8 107.0 %reduce-scatter.5.cloned.1.call-done = bf16[64,3584]{1,0:T(8,128)(2,1)} async-done(((bf16[1024,3584]{1,0:T(8,128)(2,1)}), bf16[64,3584]{1,0:T(8,128)(2,1)}) %reduce-scatter.5.cloned.1.call-update) | async-done | bytes 458768 | tf_op jit(solution)/shard_map/reduce_scatter | solution.py:139
  431.8 161.9 %reduce-scatter.3.cloned.1.call-done = bf16[64,3584]{1,0:T(8,128)(2,1)} async-done(((bf16[1024,3584]{1,0:T(8,128)(2,1)}), bf16[64,3584]{1,0:T(8,128)(2,1)}) %reduce-scatter.3.cloned.1.call-update) | async-done | bytes 458768 | tf_op jit(solution)/shard_map/reduce_scatter | solution.py:128
  (28 shorter events, 1.0 us)
Async XLA Ops:
  7.2 107.2 %all-gather.3.cloned.1.call-start = ((), (), s32[]{:S(2)}) async-start(), calls=%async_computation.4 | async-start | bytes 7798784 | tf_op jit(solution)/shard_map/all_gather | solution.py:123
  7.9 210.8 %all-gather.5.cloned.1.call-start = ((), (), s32[]{:S(2)}) async-start(), calls=%async_computation.6 | async-start | bytes 7798784 | tf_op jit(solution)/shard_map/all_gather | solution.py:124
  8.6 423.2 %reduce-scatter.5.cloned.1.call-start = ((), (), s32[]{:S(2)}) async-start(), calls=%async_computation.7 | async-start | bytes 7798784 | tf_op jit(solution)/shard_map/reduce_scatter | solution.py:139
  8.7 6.8 %collective-permute-start = (bf16[3584,512]{1,0:T(8,128)(2,1)}, bf16[3584,512]{1,0:T(8,128)(2,1)}, u32[]{:S(2)}, u32[]{:S(2)}) collective-permute-start(bf16[3584,512]{1,0:T(8,128)(2,1)} %bitcast.59), channel_id=1, source_target_pairs={{0,1},{1,0},{2,3},{3,2},{4,5},{5,4},{6,7},{7,6},{8,9},{9,8},{10,11... | collective-permute-start | bytes 11010056 | tf_op jit(solution)/shard_map/ppermute | solution.py:117
  8.8 119.1 %collective-permute-start.1 = (bf16[512,3584]{1,0:T(8,128)(2,1)}, bf16[512,3584]{1,0:T(8,128)(2,1)}, u32[]{:S(2)}, u32[]{:S(2)}) collective-permute-start(bf16[512,3584]{1,0:T(8,128)(2,1)} %bitcast.62), channel_id=1, source_target_pairs={{0,1},{1,0},{2,3},{3,2},{4,5},{5,4},{6,7},{7,6},{8,9},{9,8},{10,11... | collective-permute-start | bytes 11010056 | tf_op jit(solution)/shard_map/ppermute | solution.py:118
  127.9 115.9 %copy-start.2 = (s32[64,8]{0,1:T(8,128)S(1)}, s32[64,8]{0,1:T(8,128)}, u32[]{:S(2)}) copy-start(s32[64,8]{0,1:T(8,128)} %param.7) | copy-start | bytes 6148
  127.9 115.9 %copy-start.3 = (f32[64,8]{0,1:T(8,128)S(1)}, f32[64,8]{0,1:T(8,128)}, u32[]{:S(2)}) copy-start(f32[64,8]{0,1:T(8,128)} %param.8) | copy-start | bytes 6148
  255.5 6.9 %copy-start.4 = (bf16[1,3584,512]{2,1,0:T(8,128)(2,1)S(1)}, bf16[1,3584,512]{2,1,0:T(8,128)(2,1)}, u32[]{:S(2)}) copy-start(bf16[1,3584,512]{2,1,0:T(8,128)(2,1)} %param.10) | copy-start | bytes 11010052
  261.1 1.3 copy-start
  274.4 319.4 %reduce-scatter.3.cloned.1.call-start = ((), (), s32[]{:S(2)}) async-start(), calls=%async_computation.5 | async-start | bytes 7798784 | tf_op jit(solution)/shard_map/reduce_scatter | solution.py:128
  287.7 16.6 %slice-start = ((s8[7340032]{0:T(1024)(128)(4,1)}), s8[4194304]{0:T(1024)(128)(4,1)S(1)}, s32[]{:S(2)}) async-start(s8[7340032]{0:T(1024)(128)(4,1)} %bitcast.57), calls=%async_computation.8 | async-start | bytes 8388608
  295.3 9.1 %copy-start.1 = (bf16[1024,1024]{0,1:T(8,128)(2,1)S(1)}, bf16[1024,1024]{0,1:T(8,128)(2,1)}, u32[]{:S(2)}) copy-start(bf16[1024,1024]{0,1:T(8,128)(2,1)} %copy-done) | copy-start | bytes 6291460
  295.3 9.1 %slice-start.1 = ((s8[7340032]{0:T(1024)(128)(4,1)}), s8[3145728]{0:T(1024)(128)(4,1)S(1)}, s32[]{:S(2)}) async-start(s8[7340032]{0:T(1024)(128)(4,1)} %bitcast.57), calls=%async_computation.9 | async-start | bytes 6291456
  295.3 9.1 %collective-permute-start.2 = (bf16[3584,512]{0,1:T(8,128)(2,1)S(1)}, bf16[3584,512]{0,1:T(8,128)(2,1)S(1)}, u32[]{:S(2)}, u32[]{:S(2)}) collective-permute-start(bf16[3584,512]{0,1:T(8,128)(2,1)S(1)} %fusion.1), channel_id=1, source_target_pairs={{0,1},{1,0},{2,3},{3,2},{4,5},{5,4},{6,7},{7,6},{8,9},{9,8},{10,11... | collective-permute-start | bytes 11010056 | tf_op jit(solution)/shard_map/ppermute | solution.py:157
  304.0 11.7 %collective-permute-start.3 = (bf16[512,3584]{1,0:T(8,128)(2,1)}, bf16[512,3584]{1,0:T(8,128)(2,1)}, u32[]{:S(2)}, u32[]{:S(2)}) collective-permute-start(bf16[512,3584]{1,0:T(8,128)(2,1)} %convolution_convert_fusion.2), channel_id=1, source_target_pairs={{0,1},{1,0},{2,3},{3,2},{4,5},{5,4},{6,7},{7,6},{8,9},{9,8},{10,11... | collective-permute-start | bytes 11010056 | tf_op jit(solution)/shard_map/ppermute | solution.py:156
Sparse Core Ops, SparseCore 0:
  10.7 103.6 all-gather.2
  117.0 101.6 all-gather.4
  274.5 157.2 reduce-scatter.4
  434.6 159.1 reduce-scatter.2
where the time goes:
time: 601 us; the launch traced here: 600 us
  waiting for transfers between devices  466 us (78%)
  matrix products  84.3 us (14%)
  blocking collectives  19.9 us (3%)
  between operations  13.9 us (2%)
  local copies, waits for them, and re-layouts  7.92 us (1%)
  other arithmetic  6.87 us (1%)
    reduce_scatter x1, waiting for transfers between devices, dense_shards(): lax.psum_scatter(mixed_part.astype(jnp.bfloat16), 'expert', scatter_dimen...  162 us
    reduce_scatter x1, waiting for transfers between devices, dense_shards(): lax.psum_scatter(dx_part.astype(jnp.bfloat16), 'expert', scatter_dimensio...  107 us
    all_gather x1, waiting for transfers between devices, dense_shards(): all_x = lax.all_gather(tokens, 'expert', axis=0, tiled=True)  98.8 us
    all_gather x1, waiting for transfers between devices, dense_shards(): all_u = lax.all_gather(upstream, 'expert', axis=0, tiled=True)  90.8 us
    dot_general x4, matrix products, outer(): lax.dot_general(rows, columns, (((0,), (0,)), ((), ())), preferred_elemen...  30.7 us
    dot_general x1, matrix products, dense_shards(): lax.dot_general(all_u, down_full, (((1,), (1,)), ((), ())), preferred_ele...  15 us
    dot_general x1, matrix products, dense_shards(): hidden = jnp.dot(all_x, up_full, preferred_element_type=jnp.float32)  13.6 us
    dot_general x1, matrix products, dense_shards(): mixed_part = jnp.dot(gated, down_full, preferred_element_type=jnp.float32)  13 us
  transfers between devices with their start and end apart: 8, of which 5 were waited for; matrix products, arithmetic and copies ran while one was open for 11% of the time, Pallas kernels for 0%

commit v1 on v0

--- a/solution.py
+++ b/solution.py
@@ -120,7 +120,16 @@
     gate_of = jnp.sum(jnp.where(named, gates[:, :, None], 0.0), axis=1)
     gate = lax.all_to_all(gate_of.T, "expert", split_axis=0, concat_axis=0, tiled=True)
     gate = gate.reshape(-1)[:, None]
-    all_x = lax.all_gather(tokens, "expert", axis=0, tiled=True)
+    ways = lax.axis_size("expert")
+    up = [(d, (d + 1) % ways) for d in range(ways)]
+    down = [(d, (d - 1) % ways) for d in range(ways)]
+    earlier_2, later = ([tokens], [tokens])
+    for _ in range(ways // 2):
+        earlier_2.append(lax.ppermute(earlier_2[-1], "expert", up))
+    for _ in range((ways - 1) // 2):
+        later.append(lax.ppermute(later[-1], "expert", down))
+    line = jnp.concatenate([*earlier_2[::-1], *later[1:]], axis=0)
+    all_x = jnp.roll(line, (lax.axis_index("expert") - ways // 2) * tokens.shape[0], axis=0)
     all_u = lax.all_gather(upstream, "expert", axis=0, tiled=True)
     hidden = jnp.dot(all_x, up_full, preferred_element_type=jnp.float32)
     gated = (gate * gelu_value(hidden)).astype(jnp.bfloat16)

time: 601 us -> 644 us (1.072)
  starting transfers between devices: 1.33 us -> 49.4 us
  waiting for transfers between devices: 466 us -> 447 us
  local copies, waits for them, and re-layouts: 7.92 us -> 19.4 us
    ppermute x0 -> x15, waiting for transfers between devices: none -> 114 us  [the longest x7 67.4 us: dense_shards(): later.append(lax.ppermute(later[-1], 'expert', down))]
    all_gather x1 -> x0, waiting for transfers between devices: 98.8 us -> none  [dense_shards(): all_x = lax.all_gather(tokens, 'expert', axis=0, tiled=True)]
    ppermute x0 -> x15, starting transfers between devices: none -> 48.3 us  [the longest x8 48.3 us: dense_shards(): earlier_2.append(lax.ppermute(earlier_2[-1], 'expert', up))]
    all_gather x1, waiting for transfers between devices: 90.8 us -> 59.6 us  [dense_shards(): all_u = lax.all_gather(upstream, 'expert', axis=0, tiled=True)]
    unnamed x15 -> x69, local copies, waits for them, and re-layouts: 7.26 us -> 18.7 us
  transfers between devices with their start and end apart: 8 -> 22, of which waited for: 5 -> 16; matrix products, arithmetic and copies ran while one was open for 11% -> 11% of each run, Pallas kernels for 0% -> 0%
where the time goes in v1:
time: 644 us; the launch traced here: 643 us
  waiting for transfers between devices  447 us (69%)
  matrix products  85.2 us (13%)
  starting transfers between devices  49.4 us (8%)
  blocking collectives  19.8 us (3%)
  local copies, waits for them, and re-layouts  19.4 us (3%)
  between operations  14.2 us (2%)
  other arithmetic  7.87 us (1%)
    reduce_scatter x1, waiting for transfers between devices, dense_shards(): lax.psum_scatter(mixed_part.astype(jnp.bfloat16), 'expert', scatter_dimen...  162 us
    reduce_scatter x1, waiting for transfers between devices, dense_shards(): lax.psum_scatter(dx_part.astype(jnp.bfloat16), 'expert', scatter_dimensio...  111 us
    ppermute x7, waiting for transfers between devices, dense_shards(): later.append(lax.ppermute(later[-1], 'expert', down))  67.4 us
    all_gather x1, waiting for transfers between devices, dense_shards(): all_u = lax.all_gather(upstream, 'expert', axis=0, tiled=True)  59.6 us
    ppermute x8, starting transfers between devices, dense_shards(): earlier_2.append(lax.ppermute(earlier_2[-1], 'expert', up))  48.3 us
    ppermute x8, waiting for transfers between devices, dense_shards(): earlier_2.append(lax.ppermute(earlier_2[-1], 'expert', up))  47.1 us
    dot_general x4, matrix products, outer(): lax.dot_general(rows, columns, (((0,), (0,)), ((), ())), preferred_elemen...  33 us
    unnamed x69, local copies, waits for them, and re-layouts  18.7 us
  transfers between devices with their start and end apart: 22, of which 16 were waited for; matrix products, arithmetic and copies ran while one was open for 11% of the time, Pallas kernels for 0%

profile of v1, /device:TPU:10, one launch (start us, length us, event | category | flops | bytes accessed | tf_op | source)
XLA Modules:
  0.0 643.2 jit_solution(14309614750929760985)
XLA Ops:
  8.8 11.0 %collective-permute-done = bf16[64,3584]{1,0:T(8,128)(2,1)S(1)} collective-permute-done((bf16[64,3584]{1,0:T(8,128)(2,1)}, bf16[64,3584]{1,0:T(8,128)(2,1)S(1)}, u32[]{:S(2)}, u32[]{:S(2)}) %collective-permute-start) | collective-permute-done | bytes 458784 | tf_op jit(solution)/shard_map/ppermute | solution.py:128
  22.1 19.4 %collective-permute-done.1 = bf16[64,3584]{1,0:T(8,128)(2,1)S(1)} collective-permute-done((bf16[64,3584]{1,0:T(8,128)(2,1)S(1)}, bf16[64,3584]{1,0:T(8,128)(2,1)S(1)}, u32[]{:S(2)}, u32[]{:S(2)}) %collective-permute-start.1) | collective-permute-done | bytes 458784 | tf_op jit(solution)/shard_map/ppermute | solution.py:128
  55.9 10.3 %collective-permute-done.9 = bf16[64,3584]{1,0:T(8,128)(2,1)S(1)} collective-permute-done((bf16[64,3584]{1,0:T(8,128)(2,1)S(1)}, bf16[64,3584]{1,0:T(8,128)(2,1)S(1)}, u32[]{:S(2)}, u32[]{:S(2)}) %collective-permute-start.9) | collective-permute-done | bytes 458784 | tf_op jit(solution)/shard_map/ppermute | solution.py:130
  72.6 12.5 %collective-permute-start.4 = (bf16[64,3584]{1,0:T(8,128)(2,1)S(1)}, bf16[64,3584]{1,0:T(8,128)(2,1)S(1)}, u32[]{:S(2)}, u32[]{:S(2)}) collective-permute-start(bf16[64,3584]{1,0:T(8,128)(2,1)S(1)} %collective-permute-done.3), channel_id=1, source_target_pairs={{0,2},{2,4},{4,6},{6,8},{8,10},{10,12},{12,14},{14,16},{16,18},{18... | collective-permute-start | bytes 1376264 | tf_op jit(solution)/shard_map/ppermute | solution.py:128
  85.1 11.3 %collective-permute-done.10 = bf16[64,3584]{1,0:T(8,128)(2,1)S(1)} collective-permute-done((bf16[64,3584]{1,0:T(8,128)(2,1)S(1)}, bf16[64,3584]{1,0:T(8,128)(2,1)S(1)}, u32[]{:S(2)}, u32[]{:S(2)}) %collective-permute-start.10) | collective-permute-done | bytes 458784 | tf_op jit(solution)/shard_map/ppermute | solution.py:130
  96.3 11.0 %collective-permute-start.5 = (bf16[64,3584]{1,0:T(8,128)(2,1)S(1)}, bf16[64,3584]{1,0:T(8,128)(2,1)S(1)}, u32[]{:S(2)}, u32[]{:S(2)}) collective-permute-start(bf16[64,3584]{1,0:T(8,128)(2,1)S(1)} %collective-permute-done.4), channel_id=1, source_target_pairs={{0,2},{2,4},{4,6},{6,8},{8,10},{10,12},{12,14},{14,16},{16,18},{18... | collective-permute-start | bytes 1376264 | tf_op jit(solution)/shard_map/ppermute | solution.py:128
  107.4 11.4 %collective-permute-done.11 = bf16[64,3584]{1,0:T(8,128)(2,1)S(1)} collective-permute-done((bf16[64,3584]{1,0:T(8,128)(2,1)S(1)}, bf16[64,3584]{1,0:T(8,128)(2,1)S(1)}, u32[]{:S(2)}, u32[]{:S(2)}) %collective-permute-start.11) | collective-permute-done | bytes 458784 | tf_op jit(solution)/shard_map/ppermute | solution.py:130
  119.5 8.6 %collective-permute-start.6 = (bf16[64,3584]{1,0:T(8,128)(2,1)S(1)}, bf16[64,3584]{1,0:T(8,128)(2,1)}, u32[]{:S(2)}, u32[]{:S(2)}) collective-permute-start(bf16[64,3584]{1,0:T(8,128)(2,1)S(1)} %collective-permute-done.5), channel_id=1, source_target_pairs={{0,2},{2,4},{4,6},{6,8},{8,10},{10,12},{12,14},{14,16},{16,18},{18... | collective-permute-start | bytes 1376264 | tf_op jit(solution)/shard_map/ppermute | solution.py:128
  128.1 10.4 %collective-permute-done.12 = bf16[64,3584]{1,0:T(8,128)(2,1)} collective-permute-done((bf16[64,3584]{1,0:T(8,128)(2,1)S(1)}, bf16[64,3584]{1,0:T(8,128)(2,1)}, u32[]{:S(2)}, u32[]{:S(2)}) %collective-permute-start.12) | collective-permute-done | bytes 458784 | tf_op jit(solution)/shard_map/ppermute | solution.py:130
  138.9 8.9 %collective-permute-start.7 = (bf16[64,3584]{1,0:T(8,128)(2,1)}, bf16[64,3584]{1,0:T(8,128)(2,1)}, u32[]{:S(2)}, u32[]{:S(2)}) collective-permute-start(bf16[64,3584]{1,0:T(8,128)(2,1)} %collective-permute-done.6), channel_id=1, source_target_pairs={{0,2},{2,4},{4,6},{6,8},{8,10},{10,12},{12,14},{14,16},{16,18},{18... | collective-permute-start | bytes 1376264 | tf_op jit(solution)/shard_map/ppermute | solution.py:128
  148.4 9.8 %collective-permute-done.13 = bf16[64,3584]{1,0:T(8,128)(2,1)} collective-permute-done((bf16[64,3584]{1,0:T(8,128)(2,1)}, bf16[64,3584]{1,0:T(8,128)(2,1)}, u32[]{:S(2)}, u32[]{:S(2)}) %collective-permute-start.13) | collective-permute-done | bytes 458784 | tf_op jit(solution)/shard_map/ppermute | solution.py:130
  167.6 11.8 %collective-permute-done.14 = bf16[64,3584]{1,0:T(8,128)(2,1)S(1)} collective-permute-done((bf16[64,3584]{1,0:T(8,128)(2,1)}, bf16[64,3584]{1,0:T(8,128)(2,1)S(1)}, u32[]{:S(2)}, u32[]{:S(2)}) %collective-permute-start.14) | collective-permute-done | bytes 458784 | tf_op jit(solution)/shard_map/ppermute | solution.py:130
  189.6 12.6 %fusion.2 = f32[1024,1024]{0,1:T(8,128)} fusion(bf16[2048,3584]{1,0:T(8,128)(2,1)} %copy-done.10, s32[]{:T(128)S(6)} %select_n.23, bf16[3584,512]{1,0:T(8,128)(2,1)} %collective-permute-done.15, bf16[3584,512]{1,0:T(8,128)(2,1)S(1)} %bitcast.33), kind=kOutput, calls=%fused_computation.12 | convolution fusion | flops 7530872832 | bytes 18874372 | tf_op jit(solution)/shard_map/dot_general | solution.py:134
  202.2 59.6 %all-gather.2.cloned.1.call-done = bf16[1024,3584]{1,0:T(8,128)(2,1)} async-done(((bf16[64,3584]{1,0:T(8,128)(2,1)}), bf16[1024,3584]{1,0:T(8,128)(2,1)}) %all-gather.2.cloned.1.call-update) | async-done | bytes 7340048 | tf_op jit(solution)/shard_map/all_gather | solution.py:133
  261.8 14.9 %fusion.15 = (f32[1024]{0:T(1024)S(1)}, f32[1024,1024]{1,0:T(8,128)}) fusion(f32[1024,1024]{0,1:T(8,128)} %fusion.2, bf16[1024,3584]{1,0:T(8,128)(2,1)} %all-gather.2.cloned.1.call-done, bf16[512,3584]{1,0:T(8,128)(2,1)} %collective-permute-done.16, bf16[512,3584]{1,0:T(8,128)(2,1)} %bitcast.36), kind=kOutput, calls=%fused_computation.25 | convolution fusion | flops 7541357568 | bytes 23072768 | tf_op jit(solution)/shard_map/dot_general | solution.py:140
  276.8 10.0 %all_to_all.21 = f32[16,1,64]{2,1,0:T(1,128)S(1)} all-to-all(f32[16,1,64]{2,1,0:T(1,128)S(1)} %bitcast.29), channel_id=1, replica_groups=mesh['expert'=16,'tok'=2] {'expert'}, dimensions={0} | all-to-all | bytes 8192 | tf_op jit(solution)/shard_map/all_to_all | solution.py:151
  287.4 9.8 %all_to_all.22 = f32[16,1,64]{2,1,0:T(1,128)S(1)} all-to-all(f32[16,1,64]{2,1,0:T(1,128)S(1)} %bitcast.28), channel_id=1, replica_groups=mesh['expert'=16,'tok'=2] {'expert'}, dimensions={0} | all-to-all | bytes 8192 | tf_op jit(solution)/shard_map/all_to_all | solution.py:121
  305.1 12.0 %convolution_convert_fusion = bf16[1024,3584]{1,0:T(8,128)(2,1)} fusion(bf16[1024,1024]{0,1:T(8,128)(2,1)S(1)} %get-tuple-element.7, bf16[3584,512]{1,0:T(8,128)(2,1)} %collective-permute-done.15, bf16[3584,512]{1,0:T(8,128)(2,1)S(1)} %bitcast.34), kind=kOutput, calls=%fused_computation | convolution fusion | flops 7534542848 | bytes 16777216 | tf_op jit(solution)/shard_map/dot_general | solution.py:145
  317.2 12.8 %convolution_convert_fusion.1 = bf16[1024,3584]{1,0:T(8,128)(2,1)} fusion(bf16[1024,1024]{0,1:T(8,128)(2,1)} %get-tuple-element.8, bf16[512,3584]{1,0:T(8,128)(2,1)} %collective-permute-done.16, bf16[512,3584]{1,0:T(8,128)(2,1)} %bitcast.37), kind=kOutput, calls=%fused_computation.1 | convolution fusion | flops 7534542848 | bytes 16777216 | tf_op jit(solution)/shard_map/dot_general | solution.py:136
  330.0 9.3 %convolution_convert_fusion.2 = bf16[512,3584]{1,0:T(8,128)(2,1)} fusion(bf16[1024,3584]{1,0:T(8,128)(2,1)} %all-gather.2.cloned.1.call-done, bf16[1024,1024]{0,1:T(8,128)(2,1)} %get-tuple-element.8), kind=kOutput, calls=%fused_computation.8 | convolution fusion | flops 3759931392 | bytes 12058624 | tf_op jit(solution)/shard_map/dot_general | solution.py:157
  339.2 8.8 %convolution_convert_fusion.3 = bf16[3584,512]{1,0:T(8,128)(2,1)} fusion(bf16[2048,3584]{1,0:T(8,128)(2,1)} %copy-done.10, s32[]{:T(128)S(6)} %select_n.23, bf16[1024,1024]{0,1:T(8,128)(2,1)S(1)} %get-tuple-element.7), kind=kOutput, calls=%fused_computation.9 | convolution fusion | flops 3759931392 | bytes 12058628 | tf_op jit(solution)/shard_map/dot_general | solution.py:157
  348.5 9.2 %fusion.16 = bf16[1,512,3584]{2,1,0:T(8,128)(2,1)} fusion(bf16[512,3584]{1,0:T(8,128)(2,1)} %collective-permute-done.18, bf16[1024,3584]{1,0:T(8,128)(2,1)} %all-gather.2.cloned.1.call-done, bf16[1024,1024]{0,1:T(8,128)(2,1)S(1)} %copy-done), kind=kOutput, calls=%fused_computation.28 | convolution fusion | flops 3763601408 | bytes 15728640 | tf_op jit(solution)/shard_map/dot_general | solution.py:157
  363.5 111.1 %reduce-scatter.5.cloned.1.call-done = bf16[64,3584]{1,0:T(8,128)(2,1)} async-done(((bf16[1024,3584]{1,0:T(8,128)(2,1)}), bf16[64,3584]{1,0:T(8,128)(2,1)}) %reduce-scatter.5.cloned.1.call-update) | async-done | bytes 458768 | tf_op jit(solution)/shard_map/reduce_scatter | solution.py:148
  474.6 162.0 %reduce-scatter.3.cloned.1.call-done = bf16[64,3584]{1,0:T(8,128)(2,1)} async-done(((bf16[1024,3584]{1,0:T(8,128)(2,1)}), bf16[64,3584]{1,0:T(8,128)(2,1)}) %reduce-scatter.3.cloned.1.call-update) | async-done | bytes 458768 | tf_op jit(solution)/shard_map/reduce_scatter | solution.py:137
  (110 shorter events, 60.7 us)
Async XLA Ops:
  7.2 158.1 %copy-start.1 = (bf16[64,3584]{1,0:T(8,128)(2,1)S(1)}, bf16[64,3584]{1,0:T(8,128)(2,1)}, u32[]{:S(2)}) copy-start(bf16[64,3584]{1,0:T(8,128)(2,1)} %param.6) | copy-start | bytes 1376260
  7.2 254.6 %all-gather.2.cloned.1.call-start = ((), (), s32[]{:S(2)}) async-start(), calls=%async_computation.5 | async-start | bytes 7798784 | tf_op jit(solution)/shard_map/all_gather | solution.py:133
  7.2 12.5 %collective-permute-start = (bf16[64,3584]{1,0:T(8,128)(2,1)}, bf16[64,3584]{1,0:T(8,128)(2,1)S(1)}, u32[]{:S(2)}, u32[]{:S(2)}) collective-permute-start(bf16[64,3584]{1,0:T(8,128)(2,1)} %param.6), channel_id=1, source_target_pairs={{0,2},{2,4},{4,6},{6,8},{8,10},{10,12},{12,14},{14,16},{16,18},{18... | collective-permute-start | bytes 1376264 | tf_op jit(solution)/shard_map/ppermute | solution.py:128
  19.7 21.8 %collective-permute-start.1 = (bf16[64,3584]{1,0:T(8,128)(2,1)S(1)}, bf16[64,3584]{1,0:T(8,128)(2,1)S(1)}, u32[]{:S(2)}, u32[]{:S(2)}) collective-permute-start(bf16[64,3584]{1,0:T(8,128)(2,1)S(1)} %collective-permute-done), channel_id=1, source_target_pairs={{0,2},{2,4},{4,6},{6,8},{8,10},{10,12},{12,14},{14,16},{16,18},{18... | collective-permute-start | bytes 1376264 | tf_op jit(solution)/shard_map/ppermute | solution.py:128
  22.1 21.9 %collective-permute-start.8 = (bf16[64,3584]{1,0:T(8,128)(2,1)}, bf16[64,3584]{1,0:T(8,128)(2,1)S(1)}, u32[]{:S(2)}, u32[]{:S(2)}) collective-permute-start(bf16[64,3584]{1,0:T(8,128)(2,1)} %param.6), channel_id=1, source_target_pairs={{0,30},{2,0},{4,2},{6,4},{8,6},{10,8},{12,10},{14,12},{16,14},{18,... | collective-permute-start | bytes 1376264 | tf_op jit(solution)/shard_map/ppermute | solution.py:130
  41.6 11.0 %collective-permute-start.2 = (bf16[64,3584]{1,0:T(8,128)(2,1)S(1)}, bf16[64,3584]{1,0:T(8,128)(2,1)S(1)}, u32[]{:S(2)}, u32[]{:S(2)}) collective-permute-start(bf16[64,3584]{1,0:T(8,128)(2,1)S(1)} %collective-permute-done.1), channel_id=1, source_target_pairs={{0,2},{2,4},{4,6},{6,8},{8,10},{10,12},{12,14},{14,16},{16,18},{18... | collective-permute-start | bytes 1376264 | tf_op jit(solution)/shard_map/ppermute | solution.py:128
  44.0 22.3 %collective-permute-start.9 = (bf16[64,3584]{1,0:T(8,128)(2,1)S(1)}, bf16[64,3584]{1,0:T(8,128)(2,1)S(1)}, u32[]{:S(2)}, u32[]{:S(2)}) collective-permute-start(bf16[64,3584]{1,0:T(8,128)(2,1)S(1)} %collective-permute-done.8), channel_id=1, source_target_pairs={{0,30},{2,0},{4,2},{6,4},{8,6},{10,8},{12,10},{14,12},{16,14},{18,... | collective-permute-start | bytes 1376264 | tf_op jit(solution)/shard_map/ppermute | solution.py:130
  52.5 20.1 %collective-permute-start.3 = (bf16[64,3584]{1,0:T(8,128)(2,1)S(1)}, bf16[64,3584]{1,0:T(8,128)(2,1)S(1)}, u32[]{:S(2)}, u32[]{:S(2)}) collective-permute-start(bf16[64,3584]{1,0:T(8,128)(2,1)S(1)} %collective-permute-done.2), channel_id=1, source_target_pairs={{0,2},{2,4},{4,6},{6,8},{8,10},{10,12},{12,14},{14,16},{16,18},{18... | collective-permute-start | bytes 1376264 | tf_op jit(solution)/shard_map/ppermute | solution.py:128
  66.2 30.1 %collective-permute-start.10 = (bf16[64,3584]{1,0:T(8,128)(2,1)S(1)}, bf16[64,3584]{1,0:T(8,128)(2,1)S(1)}, u32[]{:S(2)}, u32[]{:S(2)}) collective-permute-start(bf16[64,3584]{1,0:T(8,128)(2,1)S(1)} %collective-permute-done.9), channel_id=1, source_target_pairs={{0,30},{2,0},{4,2},{6,4},{8,6},{10,8},{12,10},{14,12},{16,14},{18,... | collective-permute-start | bytes 1376264 | tf_op jit(solution)/shard_map/ppermute | solution.py:130
  72.6 23.7 %collective-permute-start.4 = (bf16[64,3584]{1,0:T(8,128)(2,1)S(1)}, bf16[64,3584]{1,0:T(8,128)(2,1)S(1)}, u32[]{:S(2)}, u32[]{:S(2)}) collective-permute-start(bf16[64,3584]{1,0:T(8,128)(2,1)S(1)} %collective-permute-done.3), channel_id=1, source_target_pairs={{0,2},{2,4},{4,6},{6,8},{8,10},{10,12},{12,14},{14,16},{16,18},{18... | collective-permute-start | bytes 1376264 | tf_op jit(solution)/shard_map/ppermute | solution.py:128
  96.3 22.4 %collective-permute-start.11 = (bf16[64,3584]{1,0:T(8,128)(2,1)S(1)}, bf16[64,3584]{1,0:T(8,128)(2,1)S(1)}, u32[]{:S(2)}, u32[]{:S(2)}) collective-permute-start(bf16[64,3584]{1,0:T(8,128)(2,1)S(1)} %collective-permute-done.10), channel_id=1, source_target_pairs={{0,30},{2,0},{4,2},{6,4},{8,6},{10,8},{12,10},{14,12},{16,14},{18,... | collective-permute-start | bytes 1376264 | tf_op jit(solution)/shard_map/ppermute | solution.py:130
  96.3 23.2 %collective-permute-start.5 = (bf16[64,3584]{1,0:T(8,128)(2,1)S(1)}, bf16[64,3584]{1,0:T(8,128)(2,1)S(1)}, u32[]{:S(2)}, u32[]{:S(2)}) collective-permute-start(bf16[64,3584]{1,0:T(8,128)(2,1)S(1)} %collective-permute-done.4), channel_id=1, source_target_pairs={{0,2},{2,4},{4,6},{6,8},{8,10},{10,12},{12,14},{14,16},{16,18},{18... | collective-permute-start | bytes 1376264 | tf_op jit(solution)/shard_map/ppermute | solution.py:128
  119.5 19.0 %collective-permute-start.12 = (bf16[64,3584]{1,0:T(8,128)(2,1)S(1)}, bf16[64,3584]{1,0:T(8,128)(2,1)}, u32[]{:S(2)}, u32[]{:S(2)}) collective-permute-start(bf16[64,3584]{1,0:T(8,128)(2,1)S(1)} %collective-permute-done.11), channel_id=1, source_target_pairs={{0,30},{2,0},{4,2},{6,4},{8,6},{10,8},{12,10},{14,12},{16,14},{18,... | collective-permute-start | bytes 1376264 | tf_op jit(solution)/shard_map/ppermute | solution.py:130
  119.5 19.4 %collective-permute-start.6 = (bf16[64,3584]{1,0:T(8,128)(2,1)S(1)}, bf16[64,3584]{1,0:T(8,128)(2,1)}, u32[]{:S(2)}, u32[]{:S(2)}) collective-permute-start(bf16[64,3584]{1,0:T(8,128)(2,1)S(1)} %collective-permute-done.5), channel_id=1, source_target_pairs={{0,2},{2,4},{4,6},{6,8},{8,10},{10,12},{12,14},{14,16},{16,18},{18... | collective-permute-start | bytes 1376264 | tf_op jit(solution)/shard_map/ppermute | solution.py:128
  138.5 19.7 %collective-permute-start.13 = (bf16[64,3584]{1,0:T(8,128)(2,1)}, bf16[64,3584]{1,0:T(8,128)(2,1)}, u32[]{:S(2)}, u32[]{:S(2)}) collective-permute-start(bf16[64,3584]{1,0:T(8,128)(2,1)} %collective-permute-done.12), channel_id=1, source_target_pairs={{0,30},{2,0},{4,2},{6,4},{8,6},{10,8},{12,10},{14,12},{16,14},{18,... | collective-permute-start | bytes 1376264 | tf_op jit(solution)/shard_map/ppermute | solution.py:130
  138.9 20.7 %collective-permute-start.7 = (bf16[64,3584]{1,0:T(8,128)(2,1)}, bf16[64,3584]{1,0:T(8,128)(2,1)}, u32[]{:S(2)}, u32[]{:S(2)}) collective-permute-start(bf16[64,3584]{1,0:T(8,128)(2,1)} %collective-permute-done.6), channel_id=1, source_target_pairs={{0,2},{2,4},{4,6},{6,8},{8,10},{10,12},{12,14},{14,16},{16,18},{18... | collective-permute-start | bytes 1376264 | tf_op jit(solution)/shard_map/ppermute | solution.py:128
  147.8 41.9 %collective-permute-start.15 = (bf16[3584,512]{1,0:T(8,128)(2,1)}, bf16[3584,512]{1,0:T(8,128)(2,1)}, u32[]{:S(2)}, u32[]{:S(2)}) collective-permute-start(bf16[3584,512]{1,0:T(8,128)(2,1)} %bitcast.32), channel_id=1, source_target_pairs={{0,1},{1,0},{2,3},{3,2},{4,5},{5,4},{6,7},{7,6},{8,9},{9,8},{10,11... | collective-permute-start | bytes 11010056 | tf_op jit(solution)/shard_map/ppermute | solution.py:117
  147.8 54.4 %collective-permute-start.16 = (bf16[512,3584]{1,0:T(8,128)(2,1)}, bf16[512,3584]{1,0:T(8,128)(2,1)}, u32[]{:S(2)}, u32[]{:S(2)}) collective-permute-start(bf16[512,3584]{1,0:T(8,128)(2,1)} %bitcast.35), channel_id=1, source_target_pairs={{0,1},{1,0},{2,3},{3,2},{4,5},{5,4},{6,7},{7,6},{8,9},{9,8},{10,11... | collective-permute-start | bytes 11010056 | tf_op jit(solution)/shard_map/ppermute | solution.py:118
  148.3 326.3 %reduce-scatter.5.cloned.1.call-start = ((), (), s32[]{:S(2)}) async-start(), calls=%async_computation.6 | async-start | bytes 7798784 | tf_op jit(solution)/shard_map/reduce_scatter | solution.py:148
  158.2 21.3 %collective-permute-start.14 = (bf16[64,3584]{1,0:T(8,128)(2,1)}, bf16[64,3584]{1,0:T(8,128)(2,1)S(1)}, u32[]{:S(2)}, u32[]{:S(2)}) collective-permute-start(bf16[64,3584]{1,0:T(8,128)(2,1)} %collective-permute-done.13), channel_id=1, source_target_pairs={{0,30},{2,0},{4,2},{6,4},{8,6},{10,8},{12,10},{14,12},{16,14},{18,... | collective-permute-start | bytes 1376264 | tf_op jit(solution)/shard_map/ppermute | solution.py:130
  202.2 84.6 %copy-start.12 = (f32[64,8]{0,1:T(8,128)S(1)}, f32[64,8]{0,1:T(8,128)}, u32[]{:S(2)}) copy-start(f32[64,8]{0,1:T(8,128)} %param.8) | copy-start | bytes 6148
  317.1 319.5 %reduce-scatter.3.cloned.1.call-start = ((), (), s32[]{:S(2)}) async-start(), calls=%async_computation.4 | async-start | bytes 7798784 | tf_op jit(solution)/shard_map/reduce_scatter | solution.py:137
  339.2 9.3 %collective-permute-start.18 = (bf16[512,3584]{1,0:T(8,128)(2,1)}, bf16[512,3584]{1,0:T(8,128)(2,1)}, u32[]{:S(2)}, u32[]{:S(2)}) collective-permute-start(bf16[512,3584]{1,0:T(8,128)(2,1)} %convolution_convert_fusion.2), channel_id=1, source_target_pairs={{0,1},{1,0},{2,3},{3,2},{4,5},{5,4},{6,7},{7,6},{8,9},{9,8},{10,11... | collective-permute-start | bytes 11010056 | tf_op jit(solution)/shard_map/ppermute | solution.py:165
  348.0 9.7 %collective-permute-start.17 = (bf16[3584,512]{1,0:T(8,128)(2,1)}, bf16[3584,512]{1,0:T(8,128)(2,1)S(1)}, u32[]{:S(2)}, u32[]{:S(2)}) collective-permute-start(bf16[3584,512]{1,0:T(8,128)(2,1)} %convolution_convert_fusion.3), channel_id=1, source_target_pairs={{0,1},{1,0},{2,3},{3,2},{4,5},{5,4},{6,7},{7,6},{8,9},{9,8},{10,11... | collective-permute-start | bytes 11010056 | tf_op jit(solution)/shard_map/ppermute | solution.py:166
  (17 other events, 383.3 us)
Sparse Core Ops, SparseCore 0:
  148.4 113.3 all-gather.1
  317.2 157.3 reduce-scatter.4
  477.5 159.1 reduce-scatter.2
